TPU v7x, 128 devices: a whole 4x4x4 slice. The times are simulated.
128 devices in a mesh: lat: 8 (over z, x_lo), lon: 16 (over y, x_hi, core).
Axes of the slice: x: 4 (x_hi: 2, x_lo: 2; x = x_hi * 2 + x_lo), y: 4, z: 4, core: 2. Of those that a mesh axis runs over, the one named last changes fastest.
Arguments:
- features: bfloat16 [128, 512, 768], P('lat', 'lon'), may hold values from -10 to 10
- grad_output: bfloat16 [128, 512, 768], P('lat', 'lon'), may hold values from -6 to 6
- qkv_weight: bfloat16 [768, 2304], P(('lat', 'lon')), may hold values from -0.5 to 0.5
- out_weight: bfloat16 [768, 768], P(('lat', 'lon')), may hold values from -0.21875 to 0.21875
Outputs:
- grad_features: bfloat16 [128, 512, 768], P('lat', 'lon')
- grad_qkv_weight: float32 [768, 2304], P(('lat', 'lon'))
- grad_out_weight: float32 [768, 768], P(('lat', 'lon'))
All inputs are finite; a program needn't handle non-finite values.
Results may differ from a plain program's by a relative error of at most 0.018.
Values may be sent and summed in bfloat16 or wider, within the bound.
A program may use at most 128 MiB of HBM per device.

v0:
```python
import math
import jax
import jax.numpy as jnp
from jax import lax
from jax.sharding import PartitionSpec as P

HEADS = 12
RADIUS = 6
QROWS = 16
QCOLS = 16
heads_together = 2


def shifted(value, axis, steps):
    count = lax.axis_size(axis)
    pairs = [(source, (source + steps) % count) for source in range(count)]
    return lax.ppermute(value, axis, pairs)


def shifted_2(value, axis, steps):
    count = lax.axis_size(axis)
    leading, last = (max(0, -steps), min(count, count - steps))
    return lax.ppermute(value, axis, [(source, source + steps) for source in range(leading, last)])


def padded(array, sides, width, wrap):
    for axis, dim in sides:
        devices, length = (lax.axis_size(axis), array.shape[dim])
        up = [(i, (i + 1) % devices) for i in range(devices if wrap else devices - 1)]
        down = [(j, i) for i, j in up]
        last = lax.slice_in_dim(array, length - width, length, axis=dim)
        leading = lax.slice_in_dim(array, 0, width, axis=dim)
        before = lax.ppermute(last, axis, up)
        after = lax.ppermute(leading, axis, down)
        array = jnp.concatenate([before, array, after], axis=dim)
    return array


def window_mask(row_first, query_rows, query_cols, key_rows, key_cols, radius, total_rows):
    q_rows = row_first + jnp.arange(query_rows, dtype=jnp.int32)
    k_rows = row_first - radius + jnp.arange(key_rows, dtype=jnp.int32)
    row_start = jnp.clip(q_rows - radius, 0, total_rows - 2 * radius - 1)
    row_valid = (k_rows[None, :] >= row_start[:, None]) & (
        k_rows[None, :] <= row_start[:, None] + 2 * radius
    )
    q_cols = jnp.arange(query_cols, dtype=jnp.int32)
    k_cols = jnp.arange(key_cols, dtype=jnp.int32)
    col_valid = (k_cols[None, :] >= q_cols[:, None]) & (
        k_cols[None, :] <= q_cols[:, None] + 2 * radius
    )
    allowed = row_valid[:, None, :, None] & col_valid[None, :, None, :]
    return allowed.reshape(query_rows * query_cols, key_rows * key_cols)


def tile_terms(queries, keys, values, grad_heads, window, head_count, head_dim):
    q_count = queries.shape[0]
    k_count = keys.shape[0]
    softmax_scale = 1.0 / math.sqrt(head_dim)
    query_h = queries.reshape(q_count, head_count, head_dim)
    key_h = keys.reshape(k_count, head_count, head_dim)
    value_h = values.reshape(k_count, head_count, head_dim)
    grad_h = grad_heads.reshape(q_count, head_count, head_dim)
    scores = (
        jnp.einsum("qhe,khe->hqk", query_h, key_h, preferred_element_type=jnp.float32)
        * softmax_scale
    )
    scores = jnp.where(window[None], scores, -jnp.inf)
    row_max = jnp.max(scores, axis=2, keepdims=True)
    exp_terms = jnp.exp(scores - row_max)
    prob_f32 = exp_terms / jnp.sum(exp_terms, axis=2, keepdims=True)
    prob_b16 = prob_f32.astype(jnp.bfloat16)
    attended = jnp.einsum(
        "hqk,khe->qhe", prob_b16, value_h, preferred_element_type=jnp.float32
    ).astype(jnp.bfloat16)
    row_term = jnp.sum(grad_h.astype(jnp.float32) * attended.astype(jnp.float32), axis=2)
    dprob = jnp.einsum("qhe,khe->hqk", grad_h, value_h, preferred_element_type=jnp.float32)
    dscore = (prob_f32 * (dprob - row_term.T[:, :, None])).astype(jnp.bfloat16)
    grad_query = jnp.einsum("hqk,khe->qhe", dscore, key_h, preferred_element_type=jnp.float32)
    grad_key = jnp.einsum("hqk,qhe->khe", dscore, query_h, preferred_element_type=jnp.float32)
    grad_value = jnp.einsum("hqk,qhe->khe", prob_b16, grad_h, preferred_element_type=jnp.float32)
    model_part = head_count * head_dim
    return (
        attended.reshape(q_count, model_part),
        grad_query.reshape(q_count, model_part),
        grad_key.reshape(k_count, model_part),
        grad_value.reshape(k_count, model_part),
    )


def turn_lon(strip_part, offset):
    return shifted(strip_part.astype(jnp.bfloat16), "lon", offset).astype(strip_part.dtype)


def turn_lat(strip_part, offset):
    return shifted_2(strip_part.astype(jnp.bfloat16), "lat", offset).astype(strip_part.dtype)


def shards(features, grad_output, qkv_weight, out_weight):
    lat_rows, lon_cols, model_width = features.shape
    radius = RADIUS
    head_dim = model_width // HEADS
    qkv_full, out_full = (
        lax.all_gather(qkv_weight, ("lat", "lon"), axis=0, tiled=True),
        lax.all_gather(out_weight, ("lat", "lon"), axis=0, tiled=True),
    )
    x_rows = features.reshape(-1, model_width)
    grad_rows = grad_output.reshape(-1, model_width)
    projected = jnp.dot(x_rows, qkv_full, preferred_element_type=jnp.float32).astype(jnp.bfloat16)
    projected = projected.reshape(lat_rows, lon_cols, 3 * model_width)
    grad_attn = lax.dot_general(
        grad_rows, out_full, (((1,), (1,)), ((), ())), preferred_element_type=jnp.float32
    )
    grad_attn = grad_attn.astype(jnp.bfloat16).reshape(lat_rows, lon_cols, model_width)
    queries = projected[..., :model_width]
    key_value = projected[..., model_width:]
    lon_wide = padded(key_value, (("lon", 1),), radius, True)
    extended = padded(lon_wide, (("lat", 0),), radius, False)
    total_rows = lat_rows * lax.axis_size("lat")
    lat_first = lax.axis_index("lat") * lat_rows
    key_rows = QROWS + 2 * radius
    key_cols = QCOLS + 2 * radius
    wide_cols = lon_cols + 2 * radius
    grad_kv = jnp.zeros((lat_rows + 2 * radius, wide_cols, 2 * model_width), jnp.float32)
    window = window_mask(lat_first + 0, QROWS, QCOLS, key_rows, key_cols, radius, total_rows)
    out_row = []
    query_row = []
    for col_index in range(lon_cols // QCOLS):
        left_col = col_index * QCOLS
        q_tile = queries[0:QROWS, left_col : left_col + QCOLS].reshape(-1, model_width)
        g_tile = grad_attn[0:QROWS, left_col : left_col + QCOLS].reshape(-1, model_width)
        kv_tile = extended[0:key_rows, left_col : left_col + key_cols].reshape(-1, 2 * model_width)
        out_parts, query_parts, key_parts, value_parts = ([], [], [], [])
        for first_head in range(0, HEADS, heads_together):
            col_low = first_head * head_dim
            col_high = col_low + heads_together * head_dim
            attended, grad_query, grad_key, grad_value = tile_terms(
                q_tile[:, col_low:col_high],
                kv_tile[:, col_low:col_high],
                kv_tile[:, model_width + col_low : model_width + col_high],
                g_tile[:, col_low:col_high],
                window,
                heads_together,
                head_dim,
            )
            out_parts.append(attended)
            query_parts.append(grad_query)
            key_parts.append(grad_key)
            value_parts.append(grad_value)
        out_row.append(jnp.concatenate(out_parts, axis=1).reshape(QROWS, QCOLS, model_width))
        query_row.append(jnp.concatenate(query_parts, axis=1).reshape(QROWS, QCOLS, model_width))
        key_part = jnp.concatenate(key_parts + value_parts, axis=1).reshape(
            key_rows, key_cols, 2 * model_width
        )
        grad_kv = grad_kv.at[0:key_rows, left_col : left_col + key_cols].add(key_part)
    out_blocks = jnp.concatenate(out_row, axis=1)
    query_blocks = jnp.concatenate(query_row, axis=1)
    from_right = turn_lon(grad_kv[:, :radius], -1)
    from_left = turn_lon(grad_kv[:, wide_cols - radius :], 1)
    middle = grad_kv[:, radius : radius + lon_cols]
    middle = middle.at[:, :radius].add(from_left)
    middle = middle.at[:, lon_cols - radius :].add(from_right)
    from_below = turn_lat(middle[:radius], -1)
    from_above = turn_lat(middle[lat_rows + radius :], 1)
    interior = middle[radius : radius + lat_rows]
    interior = interior.at[:radius].add(from_above)
    interior = interior.at[lat_rows - radius :].add(from_below)
    softmax_scale = 1.0 / math.sqrt(head_dim)
    query_all = query_blocks.reshape(-1, model_width)
    grad_query = (query_all * softmax_scale).astype(jnp.bfloat16)
    grad_key = (
        (interior[..., :model_width] * softmax_scale).astype(jnp.bfloat16).reshape(-1, model_width)
    )
    grad_value = interior[..., model_width:].astype(jnp.bfloat16).reshape(-1, model_width)
    grad_proj = jnp.concatenate([grad_query, grad_key, grad_value], axis=1)
    attended_rows = out_blocks.reshape(-1, model_width)
    grad_features = lax.dot_general(
        grad_proj, qkv_full, (((1,), (1,)), ((), ())), preferred_element_type=jnp.float32
    )
    grad_features = grad_features.astype(jnp.bfloat16).reshape(lat_rows, lon_cols, model_width)
    first_term = lax.dot_general(
        x_rows, grad_proj, (((0,), (0,)), ((), ())), preferred_element_type=jnp.float32
    )
    second_term = lax.dot_general(
        attended_rows, grad_rows, (((0,), (0,)), ((), ())), preferred_element_type=jnp.float32
    )
    my_grads = lax.psum_scatter(
        jnp.concatenate([first_term, second_term], axis=1),
        ("lat", "lon"),
        scatter_dimension=0,
        tiled=True,
    )
    return (grad_features, my_grads[:, : 3 * model_width], my_grads[:, 3 * model_width :])


def solution(mesh):
    placed = (
        P("lat", "lon", None),
        P("lat", "lon", None),
        P(("lat", "lon"), None),
        P(("lat", "lon"), None),
    )
    return jax.shard_map(
        shards,
        mesh=mesh,
        in_specs=placed,
        out_specs=(P("lat", "lon", None), P(("lat", "lon"), None), P(("lat", "lon"), None)),
        check_vma=False,
    )
```

profile of v0, /device:TPU:1, one launch (start us, length us, event | category | flops | bytes accessed | tf_op | source)
XLA Modules:
  0.0 1026.2 jit_solution(18377570423413452368)
XLA Ops:
  9.5 3.4 and.58
  13.8 194.4 %all-gather.7.cloned.1.call-done = bf16[128,6,768]{2,1,0:T(8,128)(2,1)} async-done(((bf16[1,6,768]{2,1,0:T(8,128)(2,1)}), bf16[128,6,768]{2,1,0:T(8,128)(2,1)}) %all-gather.7.cloned.1.call-update) | async-done | bytes 1179664 | tf_op jit(solution)/shard_map/all_gather | solution.py:104
  212.3 194.4 %all-gather.5.cloned.1.call-done = bf16[128,6,2304]{2,1,0:T(8,128)(2,1)} async-done(((bf16[1,6,2304]{2,1,0:T(8,128)(2,1)}), bf16[128,6,2304]{2,1,0:T(8,128)(2,1)}) %all-gather.5.cloned.1.call-update) | async-done | bytes 3538960 | tf_op jit(solution)/shard_map/all_gather | solution.py:103
  406.7 6.6 reshape.732
  413.3 4.0 convolution_convert_fusion
  417.4 2.9 collective-permute-start
  420.6 4.8 collective-permute-done
  425.4 6.1 collective-permute-done.1
  433.4 3.5 collective-permute-start.2
  475.8 3.0 pad_maximum_fusion.1
  480.9 4.8 reshape.701
  485.7 3.2 fusion.97
  492.5 2.9 exponential_reduce_fusion.4
  504.6 2.9 exponential_reduce_fusion.5
  516.9 2.9 exponential_reduce_fusion.3
  529.1 2.9 exponential_reduce_fusion.2
  544.2 3.1 fusion.98
  573.4 3.3 exponential_reduce_fusion.8
  584.9 3.4 exponential_reduce_fusion.7
  596.5 3.4 exponential_reduce_fusion.6
  727.5 2.8 constant_dynamic-update-slice_fusion.48
  730.3 2.5 slice.521
  775.0 6.3 slice.492
  788.1 7.2 scatter-add.24
  797.0 6.4 scatter-add.25
  803.4 2.9 convert.15
  807.6 4.3 collective-permute-start.6
  819.6 13.0 %collective-permute-done.7 = bf16[6,32,1536]{2,1,0:T(8,128)(2,1)S(1)} collective-permute-done((bf16[6,32,1536]{2,1,0:T(8,128)(2,1)}, bf16[6,32,1536]{2,1,0:T(8,128)(2,1)S(1)}, u32[]{:S(2)}, u32[]{:S(2)}) %collective-permute-start.7) | collective-permute-done | bytes 589856 | tf_op jit(solution)/shard_map/ppermute | solution.py:23
  834.1 4.9 convolution_bitcast_fusion
  839.0 7.2 pad_maximum_fusion
  846.3 5.2 convolution_convert_fusion.2
  851.4 162.9 %all-reduce.4.cloned.1.call-done = f32[768,3072]{0,1:T(8,128)} async-done(((f32[768,3072]{0,1:T(8,128)}), f32[768,3072]{0,1:T(8,128)}) %all-reduce.4.cloned.1.call-update) | async-done | bytes 9437200
  (659 shorter events, 328.7 us)
Async XLA Ops:
  7.2 406.1 %copy-start = (bf16[16,32,768]{2,1,0:T(8,128)(2,1)S(1)}, bf16[16,32,768]{2,1,0:T(8,128)(2,1)}, u32[]{:S(2)}) copy-start(bf16[16,32,768]{2,1,0:T(8,128)(2,1)} %param.16) | copy-start | bytes 2359300
  7.2 201.1 %all-gather.7.cloned.1.call-start = ((), (), s32[]{:S(2)}) async-start(), calls=%async_computation.1 | async-start | bytes 1585152 | tf_op jit(solution)/shard_map/all_gather | solution.py:104
  7.9 398.8 %all-gather.5.cloned.1.call-start = ((), (), s32[]{:S(2)}) async-start(), calls=%async_computation | async-start | bytes 4755456 | tf_op jit(solution)/shard_map/all_gather | solution.py:103
  8.7 1005.7 %all-reduce.4.cloned.1.call-start = ((), (), s32[]{:S(2)}) async-start(), calls=%async_computation.2 | async-start | bytes 18874368
  12.8 197.7 %copy-start.87 = (bf16[16,32,768]{2,1,0:T(8,128)(2,1)S(1)}, bf16[16,32,768]{2,1,0:T(8,128)(2,1)}, u32[]{:S(2)}) copy-start(bf16[16,32,768]{2,1,0:T(8,128)(2,1)} %param.17) | copy-start | bytes 2359300
  417.4 8.0 collective-permute-start
  420.3 11.2 %collective-permute-start.1 = (bf16[16,6,1536]{2,1,0:T(8,128)(2,1)S(1)}, bf16[16,6,1536]{2,1,0:T(8,128)(2,1)S(1)}, u32[]{:S(2)}, u32[]{:S(2)}) collective-permute-start(bf16[16,6,1536]{2,1,0:T(8,128)(2,1)S(1)} %get-tuple-element.119), channel_id=1, source_target_pairs={{1,0},{2,1},{3,2},{4,3},{5,4},{6,5},{7,6},{8,7},{9,8},{10,9},{11,1... | collective-permute-start | bytes 884744 | tf_op jit(solution)/shard_map/ppermute | solution.py:34
  433.4 40.9 %collective-permute-start.2 = (bf16[6,44,1536]{2,1,0:T(8,128)(2,1)}, bf16[6,44,1536]{2,1,0:T(8,128)(2,1)}, u32[]{:S(2)}, u32[]{:S(2)}) collective-permute-start(bf16[6,44,1536]{2,1,0:T(8,128)(2,1)} %get-tuple-element.116), channel_id=1, source_target_pairs={{0,16},{16,32},{32,48},{48,64},{64,80},{80,96},{96,112},{1,17},{17... | collective-permute-start | bytes 2433032 | tf_op jit(solution)/shard_map/ppermute | solution.py:33
  436.9 38.9 %collective-permute-start.3 = (bf16[6,44,1536]{2,1,0:T(8,128)(2,1)}, bf16[6,44,1536]{2,1,0:T(8,128)(2,1)}, u32[]{:S(2)}, u32[]{:S(2)}) collective-permute-start(bf16[6,44,1536]{2,1,0:T(8,128)(2,1)} %get-tuple-element.117), channel_id=1, source_target_pairs={{16,0},{32,16},{48,32},{64,48},{80,64},{96,80},{112,96},{17,1},{33... | collective-permute-start | bytes 2433032 | tf_op jit(solution)/shard_map/ppermute | solution.py:34
  635.5 20.0 %copy-start.14 = (bf16[2,256,784]{1,2,0:T(8,128)(2,1)}, bf16[2,256,784]{1,2,0:T(8,128)(2,1)S(1)}, u32[]{:S(2)}) copy-start(bf16[2,256,784]{1,2,0:T(8,128)(2,1)S(1)} %multiply_convert_fusion) | copy-start | bytes 2408452
  701.6 19.9 %slice-start = ((s8[5505024]{0:T(1024)(128)(4,1)}), s8[1310720]{0:T(1024)(128)(4,1)S(1)}, s32[]{:S(2)}) async-start(s8[5505024]{0:T(1024)(128)(4,1)} %bitcast.341), calls=%async_computation.3 | async-start | bytes 2621440
  711.5 7.3 copy-start.22
  713.6 7.9 slice-start.1
  733.8 51.9 %collective-permute-start.4 = (bf16[28,6,1536]{2,0,1:T(8,128)(2,1)}, bf16[28,6,1536]{2,0,1:T(8,128)(2,1)}, u32[]{:S(2)}, u32[]{:S(2)}) collective-permute-start(bf16[28,6,1536]{2,0,1:T(8,128)(2,1)} %copy.253), channel_id=1, source_target_pairs={{0,1},{1,2},{2,3},{3,4},{4,5},{5,6},{6,7},{7,8},{8,9},{9,10},{10,1... | collective-permute-start | bytes 1548296 | tf_op jit(solution)/shard_map/ppermute | solution.py:17
  734.9 18.0 %copy-start.124 = (bf16[256,2,64]{0,2,1:T(8,128)(2,1)S(1)}, bf16[256,2,64]{0,2,1:T(8,128)(2,1)}, u32[]{:S(2)}) copy-start(bf16[256,2,64]{0,2,1:T(8,128)(2,1)} %get-tuple-element.177) | copy-start | bytes 196612
  734.9 60.3 %collective-permute-start.5 = (bf16[28,6,1536]{2,0,1:T(8,128)(2,1)}, bf16[28,6,1536]{2,0,1:T(8,128)(2,1)S(1)}, u32[]{:S(2)}, u32[]{:S(2)}) collective-permute-start(bf16[28,6,1536]{2,0,1:T(8,128)(2,1)} %copy.255), channel_id=1, source_target_pairs={{0,15},{1,0},{2,1},{3,2},{4,3},{5,4},{6,5},{7,6},{8,7},{9,8},{10,9... | collective-permute-start | bytes 1548296 | tf_op jit(solution)/shard_map/ppermute | solution.py:17
  738.3 26.9 %copy-start.56 = (f32[16,16,768]{2,1,0:T(8,128)S(1)}, f32[16,16,768]{2,1,0:T(8,128)}, u32[]{:S(2)}) copy-start(f32[16,16,768]{2,1,0:T(8,128)} %constant_dynamic-update-slice_fusion.5) | copy-start | bytes 2359300
  738.3 26.9 %copy-start.121 = (f32[16,16,128]{2,1,0:T(8,128)S(1)}, f32[16,16,128]{2,1,0:T(8,128)}, u32[]{:S(2)}) copy-start(f32[16,16,128]{2,1,0:T(8,128)} %concatenate.153) | copy-start | bytes 393220
  755.4 16.9 %copy-start.129 = (bf16[16,16,128]{2,1,0:T(8,128)(2,1)S(1)}, bf16[16,16,128]{2,1,0:T(8,128)(2,1)}, u32[]{:S(2)}) copy-start(bf16[16,16,128]{2,1,0:T(8,128)(2,1)} %concatenate.195) | copy-start | bytes 196612
  765.2 7.0 copy-start.130
  765.3 7.1 copy-start.131
  765.3 7.1 copy-start.132
  765.3 7.1 copy-start.133
  765.3 7.1 copy-start.134
  765.3 7.8 copy-start.135
  765.3 8.4 copy-start.136
  765.3 9.1 copy-start.137
  775.0 8.8 copy-start.61
  806.4 6.4 copy-start.119
  806.4 6.8 copy-start.59
  807.6 10.9 %collective-permute-start.6 = (bf16[6,32,1536]{2,1,0:T(8,128)(2,1)}, bf16[6,32,1536]{2,1,0:T(8,128)(2,1)}, u32[]{:S(2)}, u32[]{:S(2)}) collective-permute-start(bf16[6,32,1536]{2,1,0:T(8,128)(2,1)} %get-tuple-element.89), channel_id=1, source_target_pairs={{0,16},{16,32},{32,48},{48,64},{64,80},{80,96},{96,112},{1,17},{17... | collective-permute-start | bytes 1769480 | tf_op jit(solution)/shard_map/ppermute | solution.py:23
  815.2 17.4 %collective-permute-start.7 = (bf16[6,32,1536]{2,1,0:T(8,128)(2,1)}, bf16[6,32,1536]{2,1,0:T(8,128)(2,1)S(1)}, u32[]{:S(2)}, u32[]{:S(2)}) collective-permute-start(bf16[6,32,1536]{2,1,0:T(8,128)(2,1)} %get-tuple-element.88), channel_id=1, source_target_pairs={{16,0},{32,16},{48,32},{64,48},{80,64},{96,80},{112,96},{17,1},{33... | collective-permute-start | bytes 1769480 | tf_op jit(solution)/shard_map/ppermute | solution.py:23
  (146 other events, 392.9 us)
Sparse Core Ops, SparseCore 0:
  9.7 198.4 all-gather.6
  210.0 196.7 all-gather.4
  846.4 167.9 all-reduce.3
where the time goes:
time: 1040 us; the launch traced here: 1030 us
  waiting for transfers between devices  580 us (56%)
  local copies, waits for them, and re-layouts  268 us (26%)
  matrix products  103 us (10%)
  other arithmetic  44.1 us (4%)
  between operations  15.9 us (2%)
  starting transfers between devices  14.7 us (1%)
    all_gather x1, waiting for transfers between devices, shards(): lax.all_gather(qkv_weight, ('lat', 'lon'), axis=0, tiled=True)  194 us
    all_gather x1, waiting for transfers between devices, shards(): lax.all_gather(out_weight, ('lat', 'lon'), axis=0, tiled=True)  194 us
    unnamed x4, waiting for transfers between devices  164 us
    unnamed x428, local copies, waits for them, and re-layouts  101 us
    concatenate x26, local copies, waits for them, and re-layouts, shards(): jnp.concatenate(key_parts + value_parts, axis=1)  36.7 us
    sub x12, matrix products, tile_terms(): exp_terms = jnp.exp(scores - row_max)  29.7 us
  transfers between devices with their start and end apart: 11, of which 8 were waited for; matrix products, arithmetic and copies ran while one was open for 11% of the time, Pallas kernels for 0%

commit v1 on v0

--- a/solution.py
+++ b/solution.py
@@ -3,12 +3,21 @@
 import jax.numpy as jnp
 from jax import lax
 from jax.sharding import PartitionSpec as P
+from jax.lax import all_to_all, axis_size
 
 HEADS = 12
 RADIUS = 6
 QROWS = 16
 QCOLS = 16
 heads_together = 2
+
+
+def post_paths(frame_in, axis_name):
+    top = axis_size(axis_name)
+    long_array = jnp.stack(top * [frame_in])
+    vec_out = all_to_all(long_array, axis_name=axis_name, split_axis=0, concat_axis=0)
+    seen_now = jnp.concatenate(vec_out, axis=0)
+    return seen_now
 
 
 def shifted(value, axis, steps):
@@ -100,7 +109,7 @@
     radius = RADIUS
     head_dim = model_width // HEADS
     qkv_full, out_full = (
-        lax.all_gather(qkv_weight, ("lat", "lon"), axis=0, tiled=True),
+        post_paths(qkv_weight, ("lat", "lon")),
         lax.all_gather(out_weight, ("lat", "lon"), axis=0, tiled=True),
     )
     x_rows = features.reshape(-1, model_width)

time: 1040 us -> 881 us (0.85)
  waiting for transfers between devices: 580 us -> 406 us
  starting transfers between devices: 14.7 us -> 28.3 us
    all_gather x1 -> x0, waiting for transfers between devices: 194 us -> none  [shards(): lax.all_gather(qkv_weight, ('lat', 'lon'), axis=0, tiled=True)]
    all_gather x1, waiting for transfers between devices: 194 us -> 216 us  [shards(): lax.all_gather(out_weight, ('lat', 'lon'), axis=0, tiled=True)]
    all_to_all x0 -> x1, starting transfers between devices: none -> 11.9 us  [post_paths(): all_to_all(long_array, axis_name=axis_name, split_axis=0, concat_axis=0)]
    unnamed x428 -> x427, local copies, waits for them, and re-layouts: 101 us -> 94.4 us
    unnamed x4 -> x3, waiting for transfers between devices: 164 us -> 163 us
  transfers between devices with their start and end apart: 11 -> 11, of which waited for: 8 -> 6; matrix products, arithmetic and copies ran while one was open for 11% -> 13% of each run, Pallas kernels for 0% -> 0%
where the time goes in v1:
time: 881 us; the launch traced here: 869 us
  waiting for transfers between devices  406 us (46%)
  local copies, waits for them, and re-layouts  272 us (31%)
  matrix products  103 us (12%)
  other arithmetic  44.1 us (5%)
  starting transfers between devices  28.3 us (3%)
  between operations  16.2 us (2%)
    all_gather x1, waiting for transfers between devices, shards(): lax.all_gather(out_weight, ('lat', 'lon'), axis=0, tiled=True)  216 us
    unnamed x3, waiting for transfers between devices  163 us
    unnamed x427, local copies, waits for them, and re-layouts  94.4 us
    concatenate x26, local copies, waits for them, and re-layouts, shards(): jnp.concatenate(key_parts + value_parts, axis=1)  36.6 us
    sub x12, matrix products, tile_terms(): exp_terms = jnp.exp(scores - row_max)  29.7 us
    convert_element_type x12, other arithmetic, tile_terms(): prob_b16 = prob_f32.astype(jnp.bfloat16)  19.6 us
    transpose x12, local copies, waits for them, and re-layouts, tile_terms(): jnp.einsum('hqk,qhe->khe', prob_b16, grad_h, preferred_element_type=jnp.f...  19 us
  transfers between devices with their start and end apart: 11, of which 6 were waited for; matrix products, arithmetic and copies ran while one was open for 13% of the time, Pallas kernels for 0%

profile of v1, /device:TPU:1, one launch (start us, length us, event | category | flops | bytes accessed | tf_op | source)
XLA Modules:
  0.0 869.3 jit_solution(5284112072988623556)
XLA Ops:
  7.2 3.4 stack.2
  10.5 11.9 %all-to-all-start = ((bf16[128,6,2304]{2,1,0:T(8,128)(2,1)}), bf16[128,6,2304]{2,1,0:T(8,128)(2,1)}, u32[]{:S(2)}, u32[]{:S(2)}) async-start(bf16[128,6,2304]{2,1,0:T(8,128)(2,1)} %stack.2), calls=%async_computation | async-start | bytes 9437184 | tf_op jit(solution)/shard_map/all_to_all | solution.py:18
  24.0 3.4 and.58
  28.3 215.9 %all-gather.3.cloned.1.call-done = bf16[128,6,768]{2,1,0:T(8,128)(2,1)} async-done(((bf16[1,6,768]{2,1,0:T(8,128)(2,1)}), bf16[128,6,768]{2,1,0:T(8,128)(2,1)}) %all-gather.3.cloned.1.call-update) | async-done | bytes 1179664 | tf_op jit(solution)/shard_map/all_gather | solution.py:113
  248.3 6.6 reshape.676
  254.9 4.0 convolution_convert_fusion
  259.0 2.9 collective-permute-start
  262.1 4.8 collective-permute-done
  266.9 7.5 collective-permute-done.1
  316.0 3.0 pad_maximum_fusion.1
  321.1 4.8 reshape.707
  325.9 3.2 fusion.97
  332.6 2.9 exponential_reduce_fusion.4
  344.8 2.9 exponential_reduce_fusion.5
  357.0 2.9 exponential_reduce_fusion.3
  369.2 2.9 exponential_reduce_fusion.2
  384.4 3.2 fusion.98
  413.5 3.3 exponential_reduce_fusion.8
  425.1 3.3 exponential_reduce_fusion.7
  436.6 3.4 exponential_reduce_fusion.6
  567.6 2.8 constant_dynamic-update-slice_fusion.48
  570.4 2.5 slice.521
  616.9 6.3 slice.492
  629.9 7.2 scatter-add.24
  638.8 6.4 scatter-add.25
  645.2 2.9 convert.15
  649.4 5.4 collective-permute-start.6
  662.6 13.8 %collective-permute-done.7 = bf16[6,32,1536]{2,1,0:T(8,128)(2,1)S(1)} collective-permute-done((bf16[6,32,1536]{2,1,0:T(8,128)(2,1)}, bf16[6,32,1536]{2,1,0:T(8,128)(2,1)S(1)}, u32[]{:S(2)}, u32[]{:S(2)}) %collective-permute-start.7) | collective-permute-done | bytes 589856 | tf_op jit(solution)/shard_map/ppermute | solution.py:32
  677.8 4.9 convolution_bitcast_fusion
  682.7 7.2 pad_maximum_fusion
  690.0 5.2 convolution_convert_fusion.2
  695.2 162.0 %all-reduce.4.cloned.1.call-done = f32[768,3072]{0,1:T(8,128)} async-done(((f32[768,3072]{0,1:T(8,128)}), f32[768,3072]{0,1:T(8,128)}) %all-reduce.4.cloned.1.call-update) | async-done | bytes 9437200
  (659 shorter events, 330.4 us)
Async XLA Ops:
  7.2 247.7 %copy-start = (bf16[16,32,768]{2,1,0:T(8,128)(2,1)S(1)}, bf16[16,32,768]{2,1,0:T(8,128)(2,1)}, u32[]{:S(2)}) copy-start(bf16[16,32,768]{2,1,0:T(8,128)(2,1)} %param.16) | copy-start | bytes 2359300
  10.5 237.7 %all-to-all-start = ((bf16[128,6,2304]{2,1,0:T(8,128)(2,1)}), bf16[128,6,2304]{2,1,0:T(8,128)(2,1)}, u32[]{:S(2)}, u32[]{:S(2)}) async-start(bf16[128,6,2304]{2,1,0:T(8,128)(2,1)} %stack.2), calls=%async_computation | async-start | bytes 9437184 | tf_op jit(solution)/shard_map/all_to_all | solution.py:18
  22.4 221.8 %all-gather.3.cloned.1.call-start = ((), (), s32[]{:S(2)}) async-start(), calls=%async_computation.1 | async-start | bytes 1585152 | tf_op jit(solution)/shard_map/all_gather | solution.py:113
  23.2 833.9 %all-reduce.4.cloned.1.call-start = ((), (), s32[]{:S(2)}) async-start(), calls=%async_computation.2 | async-start | bytes 18874368
  27.4 219.2 %copy-start.87 = (bf16[16,32,768]{2,1,0:T(8,128)(2,1)S(1)}, bf16[16,32,768]{2,1,0:T(8,128)(2,1)}, u32[]{:S(2)}) copy-start(bf16[16,32,768]{2,1,0:T(8,128)(2,1)} %param.17) | copy-start | bytes 2359300
  259.0 7.9 collective-permute-start
  261.9 12.5 %collective-permute-start.1 = (bf16[16,6,1536]{2,1,0:T(8,128)(2,1)S(1)}, bf16[16,6,1536]{2,1,0:T(8,128)(2,1)S(1)}, u32[]{:S(2)}, u32[]{:S(2)}) collective-permute-start(bf16[16,6,1536]{2,1,0:T(8,128)(2,1)S(1)} %get-tuple-element.119), channel_id=1, source_target_pairs={{1,0},{2,1},{3,2},{4,3},{5,4},{6,5},{7,6},{8,7},{9,8},{10,9},{11,1... | collective-permute-start | bytes 884744 | tf_op jit(solution)/shard_map/ppermute | solution.py:43
  276.3 39.7 %collective-permute-start.2 = (bf16[6,44,1536]{2,1,0:T(8,128)(2,1)}, bf16[6,44,1536]{2,1,0:T(8,128)(2,1)}, u32[]{:S(2)}, u32[]{:S(2)}) collective-permute-start(bf16[6,44,1536]{2,1,0:T(8,128)(2,1)} %get-tuple-element.116), channel_id=1, source_target_pairs={{0,16},{16,32},{32,48},{48,64},{64,80},{80,96},{96,112},{1,17},{17... | collective-permute-start | bytes 2433032 | tf_op jit(solution)/shard_map/ppermute | solution.py:42
  278.6 37.3 %collective-permute-start.3 = (bf16[6,44,1536]{2,1,0:T(8,128)(2,1)}, bf16[6,44,1536]{2,1,0:T(8,128)(2,1)}, u32[]{:S(2)}, u32[]{:S(2)}) collective-permute-start(bf16[6,44,1536]{2,1,0:T(8,128)(2,1)} %get-tuple-element.117), channel_id=1, source_target_pairs={{16,0},{32,16},{48,32},{64,48},{80,64},{96,80},{112,96},{17,1},{33... | collective-permute-start | bytes 2433032 | tf_op jit(solution)/shard_map/ppermute | solution.py:43
  475.7 20.0 %copy-start.14 = (bf16[2,256,784]{1,2,0:T(8,128)(2,1)}, bf16[2,256,784]{1,2,0:T(8,128)(2,1)S(1)}, u32[]{:S(2)}) copy-start(bf16[2,256,784]{1,2,0:T(8,128)(2,1)S(1)} %multiply_convert_fusion) | copy-start | bytes 2408452
  541.7 19.9 %slice-start = ((s8[5505024]{0:T(1024)(128)(4,1)}), s8[1310720]{0:T(1024)(128)(4,1)S(1)}, s32[]{:S(2)}) async-start(s8[5505024]{0:T(1024)(128)(4,1)} %bitcast.340), calls=%async_computation.3 | async-start | bytes 2621440
  551.6 7.4 copy-start.22
  553.7 7.9 slice-start.1
  573.9 53.6 %collective-permute-start.4 = (bf16[28,6,1536]{2,0,1:T(8,128)(2,1)}, bf16[28,6,1536]{2,0,1:T(8,128)(2,1)}, u32[]{:S(2)}, u32[]{:S(2)}) collective-permute-start(bf16[28,6,1536]{2,0,1:T(8,128)(2,1)} %copy.253), channel_id=1, source_target_pairs={{0,1},{1,2},{2,3},{3,4},{4,5},{5,6},{6,7},{7,8},{8,9},{9,10},{10,1... | collective-permute-start | bytes 1548296 | tf_op jit(solution)/shard_map/ppermute | solution.py:26
  576.4 18.4 %copy-start.124 = (bf16[256,2,64]{0,2,1:T(8,128)(2,1)S(1)}, bf16[256,2,64]{0,2,1:T(8,128)(2,1)}, u32[]{:S(2)}) copy-start(bf16[256,2,64]{0,2,1:T(8,128)(2,1)} %get-tuple-element.177) | copy-start | bytes 196612
  576.4 60.7 %collective-permute-start.5 = (bf16[28,6,1536]{2,0,1:T(8,128)(2,1)}, bf16[28,6,1536]{2,0,1:T(8,128)(2,1)S(1)}, u32[]{:S(2)}, u32[]{:S(2)}) collective-permute-start(bf16[28,6,1536]{2,0,1:T(8,128)(2,1)} %copy.255), channel_id=1, source_target_pairs={{0,15},{1,0},{2,1},{3,2},{4,3},{5,4},{6,5},{7,6},{8,7},{9,8},{10,9... | collective-permute-start | bytes 1548296 | tf_op jit(solution)/shard_map/ppermute | solution.py:26
  580.1 27.0 %copy-start.56 = (f32[16,16,768]{2,1,0:T(8,128)S(1)}, f32[16,16,768]{2,1,0:T(8,128)}, u32[]{:S(2)}) copy-start(f32[16,16,768]{2,1,0:T(8,128)} %constant_dynamic-update-slice_fusion.5) | copy-start | bytes 2359300
  580.1 27.0 %copy-start.121 = (f32[16,16,128]{2,1,0:T(8,128)S(1)}, f32[16,16,128]{2,1,0:T(8,128)}, u32[]{:S(2)}) copy-start(f32[16,16,128]{2,1,0:T(8,128)} %concatenate.153) | copy-start | bytes 393220
  597.2 16.9 %copy-start.129 = (bf16[16,16,128]{2,1,0:T(8,128)(2,1)S(1)}, bf16[16,16,128]{2,1,0:T(8,128)(2,1)}, u32[]{:S(2)}) copy-start(bf16[16,16,128]{2,1,0:T(8,128)(2,1)} %concatenate.195) | copy-start | bytes 196612
  607.1 7.1 copy-start.131
  607.1 7.1 copy-start.132
  607.1 7.1 copy-start.133
  607.1 7.1 copy-start.134
  607.1 7.8 copy-start.135
  607.1 8.5 copy-start.136
  607.1 9.1 %copy-start.137 = (bf16[16,16,128]{2,1,0:T(8,128)(2,1)S(1)}, bf16[16,16,128]{2,1,0:T(8,128)(2,1)}, u32[]{:S(2)}) copy-start(bf16[16,16,128]{2,1,0:T(8,128)(2,1)} %concatenate.205) | copy-start | bytes 196612
  616.9 8.8 %copy-start.61 = (bf16[784,128]{0,1:T(8,128)(2,1)S(1)}, bf16[784,128]{0,1:T(8,128)(2,1)}, u32[]{:S(2)}) copy-start(bf16[784,128]{0,1:T(8,128)(2,1)} %copy-done.60) | copy-start | bytes 602116
  648.2 7.3 copy-start.120
  648.2 7.6 copy-start.119
  648.2 8.0 copy-start.59
  649.4 12.0 %collective-permute-start.6 = (bf16[6,32,1536]{2,1,0:T(8,128)(2,1)}, bf16[6,32,1536]{2,1,0:T(8,128)(2,1)}, u32[]{:S(2)}, u32[]{:S(2)}) collective-permute-start(bf16[6,32,1536]{2,1,0:T(8,128)(2,1)} %get-tuple-element.89), channel_id=1, source_target_pairs={{0,16},{16,32},{32,48},{48,64},{64,80},{80,96},{96,112},{1,17},{17... | collective-permute-start | bytes 1769480 | tf_op jit(solution)/shard_map/ppermute | solution.py:32
  658.2 18.2 %collective-permute-start.7 = (bf16[6,32,1536]{2,1,0:T(8,128)(2,1)}, bf16[6,32,1536]{2,1,0:T(8,128)(2,1)S(1)}, u32[]{:S(2)}, u32[]{:S(2)}) collective-permute-start(bf16[6,32,1536]{2,1,0:T(8,128)(2,1)} %get-tuple-element.88), channel_id=1, source_target_pairs={{16,0},{32,16},{48,32},{64,48},{80,64},{96,80},{112,96},{17,1},{33... | collective-permute-start | bytes 1769480 | tf_op jit(solution)/shard_map/ppermute | solution.py:32
  (146 other events, 402.5 us)
Sparse Core Ops, SparseCore 0:
  25.0 219.2 all-gather.2
  690.1 166.9 all-reduce.3
